TPU v7x, 32 devices: a whole 2x2x4 slice. The times are simulated.
32 devices in a mesh: row: 8 (over z, core), col: 4 (over y, x).
Axes of the slice: x: 2, y: 2, z: 4, core: 2. Of those that a mesh axis runs over, the one named last changes fastest.
Arguments:
- matrix_tiles: float32 [10, 8, 128, 20, 4, 128], P(None, 'row', None, None, 'col'), may hold values from -60715.73 to 60715.73
Outputs:
- reduced: float32 [10, 8, 128, 20, 4, 128], P(None, 'row', None, None, 'col')
All inputs are finite; a program needn't handle non-finite values.
Results may differ from a plain program's by a relative error of at most 0.0003.
Values sent between devices are 32-bit elements; how exact they have to be, the bound alone decides.
A program may use at most 128 MiB of HBM per device.

v0:
```python
import jax
import jax.numpy as jnp
from jax import lax
from jax.sharding import PartitionSpec as P

BAND = 256
PANELS = 2


def from_root(shard, axis, root):
    mine = lax.axis_index(axis) == root
    return lax.psum(jnp.where(mine, shard, jnp.zeros_like(shard)), axis)


def multiply(first_matrix, second_matrix):
    return jnp.dot(
        first_matrix,
        second_matrix,
        precision=lax.Precision.HIGHEST,
        preferred_element_type=first_matrix.dtype,
    )


def transposed_left(first_matrix, second_matrix):
    return lax.dot_general(
        first_matrix,
        second_matrix,
        (((0,), (0,)), ((), ())),
        precision=lax.Precision.HIGHEST,
        preferred_element_type=first_matrix.dtype,
    )


def transposed_right(first_matrix, second_matrix):
    return lax.dot_general(
        first_matrix,
        second_matrix,
        (((1,), (1,)), ((), ())),
        precision=lax.Precision.HIGHEST,
        preferred_element_type=first_matrix.dtype,
    )


def lower_inverse(matrix):
    factor = jnp.linalg.cholesky(matrix)
    identity = jnp.eye(matrix.shape[0], dtype=matrix.dtype)
    return lax.linalg.triangular_solve(factor, identity, left_side=True, lower=True)


def reflector_factors(gram_matrix, top_panel):
    inverse = lower_inverse(gram_matrix)
    top_basis = transposed_right(top_panel, inverse)
    sign_values = jnp.where(jnp.diagonal(top_basis) >= 0, -1.0, 1.0).astype(top_basis.dtype)
    shifted = top_basis - jnp.diag(sign_values)
    outer_inverse = lower_inverse(transposed_left(shifted, shifted))
    kernel = transposed_left(outer_inverse, outer_inverse)
    transform = -sign_values[:, None] * multiply(shifted, kernel)
    return (inverse, sign_values, transform)


def mirror_order(pieces, block_rows, tile_size):
    stacked = jnp.stack(pieces, 0)
    stacked = stacked.reshape(len(pieces), block_rows, tile_size, stacked.shape[-1])
    return stacked.transpose(1, 0, 2, 3).reshape(-1, stacked.shape[-1])


def on_device(matrix_tiles):
    tile_shape = matrix_tiles.shape
    block_rows = tile_shape[0]
    tile_size = tile_shape[2]
    block_cols = tile_shape[3]
    row_count = block_rows * tile_size
    col_count = block_cols * tile_size
    local_block = matrix_tiles.reshape(row_count, col_count)
    row_devices = lax.axis_size("row")
    col_devices = lax.axis_size("col")
    row_ratio = row_devices // col_devices
    row_index = lax.axis_index("row")
    col_index = lax.axis_index("col")
    positions = jnp.arange(row_count, dtype=jnp.int32)
    global_rows = (
        positions // tile_size * row_devices + row_index
    ) * tile_size + positions % tile_size
    band_columns = jnp.arange(BAND, dtype=jnp.int32)
    panel_tiles = BAND // tile_size
    for panel_index in range(PANELS):
        panel_start = panel_index * BAND
        below_start = panel_start + BAND
        pieces = []
        for offset in range(panel_tiles):
            column_tile = panel_start // tile_size + offset
            local_tile = column_tile // col_devices
            source = local_block[:, local_tile * tile_size : (local_tile + 1) * tile_size]
            pieces.append(from_root(source, "col", column_tile % col_devices))
        panel_rows = jnp.concatenate(pieces, 1)
        panel_rows = jnp.where((global_rows >= below_start)[:, None], panel_rows, 0.0)
        partial_gram = transposed_left(panel_rows, panel_rows)
        gram_matrix = lax.psum(partial_gram, "row")
        blocks = []
        for offset in range(panel_tiles):
            row_tile = below_start // tile_size + offset
            local_tile = row_tile // row_devices
            source = panel_rows[local_tile * tile_size : (local_tile + 1) * tile_size]
            blocks.append(from_root(source, "row", row_tile % row_devices))
        top_panel = jnp.concatenate(blocks, 0)
        inverse, sign_values, transform = reflector_factors(gram_matrix, top_panel)
        sign_places = (global_rows[:, None] - below_start == band_columns[None, :]).astype(
            local_block.dtype
        )
        vec_rows = transposed_right(panel_rows, inverse) - sign_places * sign_values[None, :]
        pieces = []
        for part_index in range(row_ratio):
            pieces.append(from_root(vec_rows, "row", col_index + col_devices * part_index))
        vec_cols = mirror_order(pieces, block_rows, tile_size)
        summed_rows = lax.psum(multiply(local_block, vec_cols), "col")
        applied = multiply(summed_rows, transform)
        inner_term = multiply(transform.T, lax.psum(transposed_left(vec_rows, applied), "row"))
        update_rows = applied - 0.5 * multiply(vec_rows, inner_term)
        column_part = transposed_left(local_block, vec_rows)
        summed_cols = lax.psum(column_part, "row")
        update_cols = multiply(summed_cols, transform) - 0.5 * multiply(vec_cols, inner_term)
        left_factor = jnp.concatenate([vec_rows, update_rows], 1)
        right_factor = jnp.concatenate([update_cols, vec_cols], 1)
        local_block = local_block - transposed_right(left_factor, right_factor)
    return local_block.reshape(tile_shape)


def solution(mesh):
    return jax.shard_map(
        on_device,
        mesh=mesh,
        in_specs=(P(None, "row", None, None, "col", None),),
        out_specs=P(None, "row", None, None, "col", None),
        check_vma=False,
    )
```

profile of v0, /device:TPU:0, one launch (start us, length us, event | category | flops | bytes accessed | tf_op | source)
XLA Modules:
  0.0 1142.7 jit_solution(3032368912725932266)
XLA Ops:
  6.5 102.2 %reduce.8 = f32[10,128,20,128]{3,2,1,0:T(8,128)} reduce(f32[10,1,128,20,1,128]{5,4,3,2,1,0:T(1,128)} %param.4, f32[]{:T(128)} %constant.208), dimensions={1,4}, to_apply=%param.4.reduce_sub_computation | reduce | bytes 26214404 | tf_op args[0]
  108.8 13.6 %copy.28 = f32[160,8,20,128]{3,1,2,0:T(8,128)} copy(f32[160,8,20,128]{3,2,1,0:T(8,128)} %bitcast.198) | data formatting | bytes 26214400
  124.7 59.2 %all-reduce.38.cloned.1.call-done = (f32[1280,128]{1,0:T(8,128)}, f32[1280,128]{1,0:T(8,128)}) async-done(((f32[1280,128]{1,0:T(8,128)}, f32[1280,128]{1,0:T(8,128)}), (f32[1280,128]{1,0:T(8,128)}, f32[1280,128]{1,0:T(8,128)})) %all-reduce.38.cloned.1.call-update) | async-done | bytes 1310736 | tf_op jit(solution)/shard_map/psum | solution.py:12
  185.4 3.0 fusion.104
  189.5 56.5 %all-reduce.34.cloned.1.call-done = (f32[128,256]{1,0:T(8,128)}, f32[128,256]{1,0:T(8,128)}, f32[256,256]{0,1:T(8,128)}) async-done(((f32[128,256]{1,0:T(8,128)}, f32[128,256]{1,0:T(8,128)}, f32[256,256]{0,1:T(8,128)}), (f32[128,256]{1,0:T(8,128)}, f32[128,256]{1,0:T(8,128)}, f32[256,256]{0,1:T(8,128)})) %all-reduce.34.cloned.1.call-update) | async-done | bytes 524304 | tf_op jit(solution)/shard_map/psum | solution.py:12
  248.1 11.7 %cholesky.214 = f32[128,128]{1,0:T(8,128)S(1)} custom-call(f32[128,128]{1,0:T(8,128)S(1)} %cholesky.346), custom_call_target="Cholesky" | custom-call | tf_op jit(solution)/shard_map/jit(cholesky)/cholesky | solution.py:45
  259.9 9.8 custom-call.21
  270.2 11.7 %cholesky.231 = f32[128,128]{1,0:T(8,128)S(1)} custom-call(f32[128,128]{1,0:T(8,128)S(1)} %convolution_subtract_fusion.11), custom_call_target="Cholesky" | custom-call | tf_op jit(solution)/shard_map/jit(cholesky)/cholesky | solution.py:45
  284.0 4.1 while.8
  288.1 19.7 %custom-call.22 = f32[2,128,128]{1,2,0:T(8,128)S(1)} custom-call(f32[2,128,128]{2,1,0:T(8,128)S(1)} %get-tuple-element.33), custom_call_target="InvertDiagBlocksLowerTriangular" | custom-call | tf_op jit(solution)/shard_map/triangular_solve/custom-call.0 | solution.py:47
  309.1 11.1 gather_fusion
  321.1 11.7 %cholesky.248 = f32[128,128]{1,0:T(8,128)S(1)} custom-call(f32[128,128]{1,0:T(8,128)S(1)} %cholesky.349), custom_call_target="Cholesky" | custom-call | tf_op jit(solution)/shard_map/jit(cholesky)/cholesky | solution.py:45
  332.9 9.8 custom-call.23
  343.2 11.7 %cholesky.265 = f32[128,128]{1,0:T(8,128)S(1)} custom-call(f32[128,128]{1,0:T(8,128)S(1)} %convolution_subtract_fusion.10), custom_call_target="Cholesky" | custom-call | tf_op jit(solution)/shard_map/jit(cholesky)/cholesky | solution.py:45
  357.6 3.6 broadcast_select_fusion.3
  361.3 4.1 while.9
  365.4 19.7 %custom-call.24 = f32[2,128,128]{1,2,0:T(8,128)S(1)} custom-call(f32[2,128,128]{2,1,0:T(8,128)S(1)} %get-tuple-element.34), custom_call_target="InvertDiagBlocksLowerTriangular" | custom-call | tf_op jit(solution)/shard_map/triangular_solve/custom-call.0 | solution.py:47
  385.7 44.1 %all-reduce.32.cloned.1.call-done = (f32[1,10,128,256]{3,2,0,1:T(8,128)}, f32[1,10,128,256]{3,2,0,1:T(8,128)}) async-done(((f32[1,10,128,256]{3,2,0,1:T(8,128)}, f32[1,10,128,256]{3,2,0,1:T(8,128)}), (f32[1,10,128,256]{3,2,0,1:T(8,128)}, f32[1,10,128,256]{3,2,0,1:T(8,128)})) %all-reduce.32.cloned.1.call-update) | async-done | bytes 2621456 | tf_op jit(solution)/shard_map/psum | solution.py:12
  431.7 25.7 %convolution_bitcast_fusion.1 = f32[1280,256]{0,1:T(8,128)} fusion(f32[2560,256]{1,0:T(8,128)S(1)} %bitcast.202, f32[1280,2560]{1,0:T(8,128)} %bitcast.193), kind=kOutput, calls=%fused_computation.30 | convolution fusion | flops 10066329600 | bytes 17039360 | tf_op jit(solution)/shard_map/dot_general | solution.py:16
  458.9 15.8 %convolution_bitcast_fusion = f32[2560,256]{0,1:T(8,128)} fusion(f32[1280,256]{1,0:T(8,128)S(1)} %copy-done.4, f32[1280,2560]{1,0:T(8,128)} %bitcast.194), kind=kOutput, calls=%fused_computation.23 | convolution fusion | flops 10066329600 | bytes 17039360 | tf_op jit(solution)/shard_map/dot_general | solution.py:25
  474.8 38.4 %all-reduce.20.cloned.1.call-done = f32[1280,256]{0,1:T(8,128)} async-done(((f32[1280,256]{0,1:T(8,128)}), f32[1280,256]{0,1:T(8,128)}) %all-reduce.20.cloned.1.call-update) | async-done | bytes 1310736 | tf_op jit(solution)/shard_map/psum | solution.py:115
  517.1 3.0 fusion.106
  523.2 69.6 %all-reduce.30.cloned.1.call-done = (f32[2560,256]{0,1:T(8,128)}, f32[256,256]{1,0:T(8,128)}) async-done(((f32[2560,256]{0,1:T(8,128)}, f32[256,256]{1,0:T(8,128)}), (f32[2560,256]{0,1:T(8,128)}, f32[256,256]{1,0:T(8,128)})) %all-reduce.30.cloned.1.call-update) | async-done | bytes 2883600 | tf_op jit(solution)/shard_map/psum | solution.py:120
  594.4 6.1 fusion.108
  604.0 24.8 %convolution_subtract_fusion.1 = f32[1280,2560]{1,0:T(8,128)S(1)} fusion(f32[1280,2560]{1,0:T(8,128)} %bitcast.195, f32[2560,256]{1,0:T(8,128)S(1)} %bitcast.204, f32[2560,256]{1,0:T(8,128)S(1)} %fusion.7, f32[1280,256]{1,0:T(8,128)S(1)} %fusion.9, f32[1280,256]{1,0:T(8,128)S(1)} %copy-done.6), kind=kOutput, calls=%fused_computation.11 | convolution fusion | flops 20137902080 | bytes 34078720 | tf_op jit(solution)/shard_map/dot_general | solution.py:35
  628.8 4.9 copy-done
  635.0 56.0 %all-reduce.36.cloned.1.call-done = (f32[1280,128]{1,0:T(8,128)}, f32[1280,128]{1,0:T(8,128)}) async-done(((f32[1280,128]{1,0:T(8,128)}, f32[1280,128]{1,0:T(8,128)}), (f32[1280,128]{1,0:T(8,128)}, f32[1280,128]{1,0:T(8,128)})) %all-reduce.36.cloned.1.call-update) | async-done | bytes 1310736 | tf_op jit(solution)/shard_map/psum | solution.py:12
  696.5 56.6 %all-reduce.28.cloned.1.call-done = (f32[128,256]{1,0:T(8,128)}, f32[128,256]{1,0:T(8,128)}, f32[256,256]{0,1:T(8,128)}) async-done(((f32[128,256]{1,0:T(8,128)}, f32[128,256]{1,0:T(8,128)}, f32[256,256]{0,1:T(8,128)}), (f32[128,256]{1,0:T(8,128)}, f32[128,256]{1,0:T(8,128)}, f32[256,256]{0,1:T(8,128)})) %all-reduce.28.cloned.1.call-update) | async-done | bytes 524304 | tf_op jit(solution)/shard_map/psum | solution.py:12
  755.2 11.7 %cholesky.282 = f32[128,128]{1,0:T(8,128)S(1)} custom-call(f32[128,128]{1,0:T(8,128)S(1)} %cholesky.352), custom_call_target="Cholesky" | custom-call | tf_op jit(solution)/shard_map/jit(cholesky)/cholesky | solution.py:45
  767.0 9.8 custom-call.25
  777.3 11.7 %cholesky.299 = f32[128,128]{1,0:T(8,128)S(1)} custom-call(f32[128,128]{1,0:T(8,128)S(1)} %convolution_subtract_fusion.9), custom_call_target="Cholesky" | custom-call | tf_op jit(solution)/shard_map/jit(cholesky)/cholesky | solution.py:45
  791.7 4.1 while.10
  795.8 19.7 %custom-call.26 = f32[2,128,128]{1,2,0:T(8,128)S(1)} custom-call(f32[2,128,128]{2,1,0:T(8,128)S(1)} %get-tuple-element.35), custom_call_target="InvertDiagBlocksLowerTriangular" | custom-call | tf_op jit(solution)/shard_map/triangular_solve/custom-call.0 | solution.py:47
  820.2 11.7 %cholesky.316 = f32[128,128]{1,0:T(8,128)S(1)} custom-call(f32[128,128]{1,0:T(8,128)S(1)} %cholesky.355), custom_call_target="Cholesky" | custom-call | tf_op jit(solution)/shard_map/jit(cholesky)/cholesky | solution.py:45
  832.0 9.8 custom-call.27
  842.3 11.7 %cholesky.333 = f32[128,128]{1,0:T(8,128)S(1)} custom-call(f32[128,128]{1,0:T(8,128)S(1)} %convolution_subtract_fusion.8), custom_call_target="Cholesky" | custom-call | tf_op jit(solution)/shard_map/jit(cholesky)/cholesky | solution.py:45
  855.4 3.6 broadcast_select_fusion.1
  860.4 4.2 while.11
  864.6 19.7 %custom-call.28 = f32[2,128,128]{1,2,0:T(8,128)S(1)} custom-call(f32[2,128,128]{2,1,0:T(8,128)S(1)} %get-tuple-element.36), custom_call_target="InvertDiagBlocksLowerTriangular" | custom-call | tf_op jit(solution)/shard_map/triangular_solve/custom-call.0 | solution.py:47
  884.9 44.1 %all-reduce.26.cloned.1.call-done = (f32[1,10,128,256]{3,2,0,1:T(8,128)}, f32[1,10,128,256]{3,2,0,1:T(8,128)}) async-done(((f32[1,10,128,256]{3,2,0,1:T(8,128)}, f32[1,10,128,256]{3,2,0,1:T(8,128)}), (f32[1,10,128,256]{3,2,0,1:T(8,128)}, f32[1,10,128,256]{3,2,0,1:T(8,128)})) %all-reduce.26.cloned.1.call-update) | async-done | bytes 2621456 | tf_op jit(solution)/shard_map/psum | solution.py:12
  930.9 14.3 %fusion.110 = f32[1280,256]{1,0:T(8,128)} fusion(f32[1280,2560]{1,0:T(8,128)} %copy-done, f32[2560,256]{1,0:T(8,128)S(1)} %bitcast.199), kind=kOutput, calls=%fused_computation.223 | convolution fusion | flops 10066329600 | bytes 17039360 | tf_op jit(solution)/shard_map/dot_general | solution.py:16
  946.6 25.0 %fusion.114 = f32[2560,256]{1,0:T(8,128)} fusion(f32[1280,2560]{1,0:T(8,128)} %copy-done, f32[1280,256]{1,0:T(8,128)S(1)} %copy-done.1), kind=kOutput, calls=%fused_computation.227 | convolution fusion | flops 10066329600 | bytes 17039360 | tf_op jit(solution)/shard_map/dot_general | solution.py:25
  971.7 29.2 %all-reduce.22.cloned.1.call-done = f32[1280,256]{1,0:T(8,128)} async-done(((f32[1280,256]{1,0:T(8,128)}), f32[1280,256]{1,0:T(8,128)}) %all-reduce.22.cloned.1.call-update) | async-done | bytes 1310736 | tf_op jit(solution)/shard_map/psum | solution.py:115
  1004.8 3.0 fusion.112
  1010.6 69.9 %all-reduce.24.cloned.1.call-done = (f32[2560,256]{1,0:T(8,128)}, f32[256,256]{1,0:T(8,128)}) async-done(((f32[2560,256]{1,0:T(8,128)}, f32[256,256]{1,0:T(8,128)}), (f32[2560,256]{1,0:T(8,128)}, f32[256,256]{1,0:T(8,128)})) %all-reduce.24.cloned.1.call-update) | async-done | bytes 2883600 | tf_op jit(solution)/shard_map/psum | solution.py:120
  1082.1 4.2 fusion.115
  1089.8 25.8 %convolution_subtract_fusion = f32[1280,2560]{1,0:T(8,128)} fusion(f32[1280,2560]{1,0:T(8,128)} %copy-done, f32[2560,256]{1,0:T(8,128)S(1)} %bitcast.201, f32[2560,256]{1,0:T(8,128)S(1)} %fusion.6, f32[1280,256]{1,0:T(8,128)S(1)} %fusion.8, f32[1280,256]{1,0:T(8,128)S(1)} %copy-done.3), kind=kOutput, calls=%fused_computation.10 | convolution fusion | flops 20137902080 | bytes 34078720 | tf_op jit(solution)/shard_map/dot_general | solution.py:35
  1115.6 19.9 %reshape.157 = f32[10,1,128,20,1,128]{5,4,3,2,1,0:T(1,128)} reshape(f32[1280,2560]{1,0:T(8,128)} %convolution_subtract_fusion) | data formatting | bytes 26214400 | tf_op jit(solution)/shard_map/reshape | solution.py:125
  (170 shorter events, 77.6 us)
Async XLA Ops:
  6.5 177.3 %all-reduce.38.cloned.1.call-start = ((), (), s32[]{:S(2)}) async-start(), calls=%async_computation.9 | async-start | bytes 2621440 | tf_op jit(solution)/shard_map/psum | solution.py:12
  124.6 121.4 %all-reduce.34.cloned.1.call-start = ((), (), s32[]{:S(2)}) async-start(), calls=%async_computation.7 | async-start | bytes 1048576 | tf_op jit(solution)/shard_map/psum | solution.py:12
  189.1 240.6 %all-reduce.32.cloned.1.call-start = ((), (), s32[]{:S(2)}) async-start(), calls=%async_computation.6 | async-start | bytes 5242880 | tf_op jit(solution)/shard_map/psum | solution.py:12
  281.9 26.7 %copy-start.11 = (f32[128,256]{1,0:T(8,128)S(1)}, f32[128,256]{1,0:T(8,128)}, u32[]{:S(2)}) copy-start(f32[128,256]{1,0:T(8,128)} %get-tuple-element.80) | copy-start | bytes 393220
  281.9 26.7 %copy-start.12 = (f32[128,256]{1,0:T(8,128)S(1)}, f32[128,256]{1,0:T(8,128)}, u32[]{:S(2)}) copy-start(f32[128,256]{1,0:T(8,128)} %get-tuple-element.81) | copy-start | bytes 393220
  361.2 152.0 %all-reduce.20.cloned.1.call-start = ((), (), s32[]{:S(2)}) async-start(), calls=%async_computation | async-start | bytes 2621440 | tf_op jit(solution)/shard_map/psum | solution.py:115
  457.5 135.3 %all-reduce.30.cloned.1.call-start = ((), (), s32[]{:S(2)}) async-start(), calls=%async_computation.5 | async-start | bytes 5767168 | tf_op jit(solution)/shard_map/psum | solution.py:120
  457.6 1.4 copy-start.4
  513.2 3.9 copy-start.5
  516.0 1.1 copy-start.7
  520.1 170.8 %all-reduce.36.cloned.1.call-start = ((), (), s32[]{:S(2)}) async-start(), calls=%async_computation.8 | async-start | bytes 2621440 | tf_op jit(solution)/shard_map/psum | solution.py:12
  594.3 6.2 copy-start.6
  594.4 6.2 copy-start.9
  628.8 5.0 copy-start
  634.9 118.2 %all-reduce.28.cloned.1.call-start = ((), (), s32[]{:S(2)}) async-start(), calls=%async_computation.4 | async-start | bytes 1048576 | tf_op jit(solution)/shard_map/psum | solution.py:12
  696.2 232.7 %all-reduce.26.cloned.1.call-start = ((), (), s32[]{:S(2)}) async-start(), calls=%async_computation.3 | async-start | bytes 5242880 | tf_op jit(solution)/shard_map/psum | solution.py:12
  789.0 27.3 %copy-start.13 = (f32[128,256]{1,0:T(8,128)S(1)}, f32[128,256]{1,0:T(8,128)}, u32[]{:S(2)}) copy-start(f32[128,256]{1,0:T(8,128)} %get-tuple-element.73) | copy-start | bytes 393220
  789.0 27.3 %copy-start.14 = (f32[128,256]{1,0:T(8,128)S(1)}, f32[128,256]{1,0:T(8,128)}, u32[]{:S(2)}) copy-start(f32[128,256]{1,0:T(8,128)} %get-tuple-element.74) | copy-start | bytes 393220
  860.3 140.5 %all-reduce.22.cloned.1.call-start = ((), (), s32[]{:S(2)}) async-start(), calls=%async_computation.1 | async-start | bytes 2621440 | tf_op jit(solution)/shard_map/psum | solution.py:115
  945.2 135.3 %all-reduce.24.cloned.1.call-start = ((), (), s32[]{:S(2)}) async-start(), calls=%async_computation.2 | async-start | bytes 5767168 | tf_op jit(solution)/shard_map/psum | solution.py:120
  945.3 1.4 copy-start.1
  1000.9 3.9 copy-start.2
  1003.7 1.1 copy-start.8
  1082.0 4.2 copy-start.3
  1082.0 4.2 copy-start.10
Sparse Core Ops, SparseCore 0:
  124.7 59.0 all-reduce.37
  189.3 56.7 all-reduce.33
  361.3 68.3 all-reduce.31
  457.6 55.5 all-reduce.19
  520.3 72.4 all-reduce.29
  635.0 55.8 all-reduce.35
  696.3 56.7 all-reduce.27
  860.5 68.4 all-reduce.25
  945.3 55.5 all-reduce.21
  1008.0 72.4 all-reduce.23
where the time goes:
time: 1150 us; the launch traced here: 1140 us
  waiting for transfers between devices  524 us (46%)
  other arithmetic  333 us (29%)
  matrix products  186 us (16%)
  local copies, waits for them, and re-layouts  78.6 us (7%)
  between operations  19.9 us (2%)
    psum x6, waiting for transfers between devices, from_root(): return lax.psum(jnp.where(mine, shard, jnp.zeros_like(shard)), axis)  316 us
    psum x2, waiting for transfers between devices, on_device(): summed_cols = lax.psum(column_part, 'row')  139 us
    another operation x27, other arithmetic, lower_inverse(): factor = jnp.linalg.cholesky(matrix)  138 us
    unnamed x1, other arithmetic  102 us
    another operation x9, other arithmetic, lower_inverse(): lax.linalg.triangular_solve(factor, identity, left_side=True, lower=True)  78.8 us
    psum x2, waiting for transfers between devices, on_device(): summed_rows = lax.psum(multiply(local_block, vec_cols), 'col')  67.6 us
    dot_general x14, matrix products, multiply(): jnp.dot(first_matrix, second_matrix, precision=lax.Precision.HIGHEST, pre...  66.7 us
    dot_general x6, matrix products, transposed_right(): lax.dot_general(first_matrix, second_matrix, (((1,), (1,)), ((), ())), pr...  58.7 us
  transfers between devices with their start and end apart: 10, of which 10 were waited for; matrix products, arithmetic and copies ran while one was open for 9% of the time, Pallas kernels for 0%

commit v1 on v0

--- a/solution.py
+++ b/solution.py
@@ -117,7 +117,13 @@
         inner_term = multiply(transform.T, lax.psum(transposed_left(vec_rows, applied), "row"))
         update_rows = applied - 0.5 * multiply(vec_rows, inner_term)
         column_part = transposed_left(local_block, vec_rows)
-        summed_cols = lax.psum(column_part, "row")
+        size = lax.axis_size("row")
+        summed_cols, stride = (column_part, 1)
+        while stride < size:
+            summed_cols = summed_cols + lax.ppermute(
+                summed_cols, "row", [(i, i ^ stride) for i in range(size)]
+            )
+            stride = 2 * stride
         update_cols = multiply(summed_cols, transform) - 0.5 * multiply(vec_cols, inner_term)
         left_factor = jnp.concatenate([vec_rows, update_rows], 1)
         right_factor = jnp.concatenate([update_cols, vec_cols], 1)

time: 1150 us -> 1260 us (1.096)
  waiting for transfers between devices: 524 us -> 603 us
  other arithmetic: 333 us -> 355 us
    psum x2, waiting for transfers between devices: 139 us -> 229 us  [on_device(): lax.psum(transposed_left(vec_rows, applied), 'row')]
    psum x2, waiting for transfers between devices: 67.6 us -> 44.1 us  [on_device(): summed_rows = lax.psum(multiply(local_block, vec_cols), 'col')]
    add x0 -> x4, other arithmetic: none -> 16.4 us  [on_device(): summed_cols + lax.ppermute(summed_cols, 'row', [(i, i ^ stride) for i in...]
    psum x6, waiting for transfers between devices: 316 us -> 330 us  [from_root(): return lax.psum(jnp.where(mine, shard, jnp.zeros_like(shard)), axis)]
  transfers between devices with their start and end apart: 10 -> 16, of which waited for: 10 -> 10; matrix products, arithmetic and copies ran while one was open for 9% -> 18% of each run, Pallas kernels for 0% -> 0%
where the time goes in v1:
time: 1260 us; the launch traced here: 1250 us
  waiting for transfers between devices  603 us (48%)
  other arithmetic  355 us (28%)
  matrix products  189 us (15%)
  local copies, waits for them, and re-layouts  73.9 us (6%)
  between operations  19.5 us (2%)
    psum x6, waiting for transfers between devices, from_root(): return lax.psum(jnp.where(mine, shard, jnp.zeros_like(shard)), axis)  330 us
    psum x2, waiting for transfers between devices, on_device(): lax.psum(transposed_left(vec_rows, applied), 'row')  229 us
    another operation x27, other arithmetic, lower_inverse(): factor = jnp.linalg.cholesky(matrix)  138 us
    unnamed x1, other arithmetic  102 us
    another operation x9, other arithmetic, lower_inverse(): lax.linalg.triangular_solve(factor, identity, left_side=True, lower=True)  82.8 us
    dot_general x14, matrix products, multiply(): jnp.dot(first_matrix, second_matrix, precision=lax.Precision.HIGHEST, pre...  72.5 us
    dot_general x6, matrix products, transposed_right(): lax.dot_general(first_matrix, second_matrix, (((1,), (1,)), ((), ())), pr...  57 us
    dot_general x10, matrix products, transposed_left(): lax.dot_general(first_matrix, second_matrix, (((0,), (0,)), ((), ())), pr...  54 us
  transfers between devices with their start and end apart: 16, of which 10 were waited for; matrix products, arithmetic and copies ran while one was open for 18% of the time, Pallas kernels for 0%

profile of v1, /device:TPU:0, one launch (start us, length us, event | category | flops | bytes accessed | tf_op | source)
XLA Modules:
  0.0 1249.1 jit_solution(12088873547385641688)
XLA Ops:
  6.5 102.2 %reduce.8 = f32[10,128,20,128]{3,2,1,0:T(8,128)} reduce(f32[10,1,128,20,1,128]{5,4,3,2,1,0:T(1,128)} %param.4, f32[]{:T(128)} %constant.208), dimensions={1,4}, to_apply=%param.4.reduce_sub_computation | reduce | bytes 26214404 | tf_op args[0]
  108.8 13.6 %copy.28 = f32[160,8,20,128]{3,1,2,0:T(8,128)} copy(f32[160,8,20,128]{3,2,1,0:T(8,128)} %bitcast.196) | data formatting | bytes 26214400
  124.7 59.2 %all-reduce.36.cloned.1.call-done = (f32[1280,128]{1,0:T(8,128)}, f32[1280,128]{1,0:T(8,128)}) async-done(((f32[1280,128]{1,0:T(8,128)}, f32[1280,128]{1,0:T(8,128)}), (f32[1280,128]{1,0:T(8,128)}, f32[1280,128]{1,0:T(8,128)})) %all-reduce.36.cloned.1.call-update) | async-done | bytes 1310736 | tf_op jit(solution)/shard_map/psum | solution.py:12
  189.4 56.6 %all-reduce.32.cloned.1.call-done = (f32[128,256]{1,0:T(8,128)}, f32[128,256]{1,0:T(8,128)}, f32[256,256]{0,1:T(8,128)}) async-done(((f32[128,256]{1,0:T(8,128)}, f32[128,256]{1,0:T(8,128)}, f32[256,256]{0,1:T(8,128)}), (f32[128,256]{1,0:T(8,128)}, f32[128,256]{1,0:T(8,128)}, f32[256,256]{0,1:T(8,128)})) %all-reduce.32.cloned.1.call-update) | async-done | bytes 524304 | tf_op jit(solution)/shard_map/psum | solution.py:12
  248.1 11.7 cholesky.214
  259.9 9.8 custom-call.21
  270.2 11.7 cholesky.231
  284.0 4.1 while.8
  288.2 19.7 %custom-call.22 = f32[2,128,128]{1,2,0:T(8,128)S(1)} custom-call(f32[2,128,128]{2,1,0:T(8,128)S(1)} %get-tuple-element.33), custom_call_target="InvertDiagBlocksLowerTriangular" | custom-call | tf_op jit(solution)/shard_map/triangular_solve/custom-call.0 | solution.py:47
  314.4 15.1 %convolution_bitcast_fusion = f32[2560,256]{0,1:T(8,128)S(1)} fusion(f32[1280,256]{1,0:T(8,128)S(1)} %get-tuple-element.125, f32[1280,2560]{1,0:T(8,128)} %bitcast.191), kind=kOutput, calls=%fused_computation.23 | convolution fusion | flops 10066329600 | bytes 17039360 | tf_op jit(solution)/shard_map/dot_general | solution.py:25
  333.3 11.7 cholesky.248
  345.1 9.8 custom-call.23
  355.0 3.8 add.166
  359.9 11.7 cholesky.265
  375.1 50.7 %all-reduce.30.cloned.1.call-done = (f32[1,10,128,256]{3,2,0,1:T(8,128)}, f32[1,10,128,256]{3,2,0,1:T(8,128)}) async-done(((f32[1,10,128,256]{3,2,0,1:T(8,128)}, f32[1,10,128,256]{3,2,0,1:T(8,128)}), (f32[1,10,128,256]{3,2,0,1:T(8,128)}, f32[1,10,128,256]{3,2,0,1:T(8,128)})) %all-reduce.30.cloned.1.call-update) | async-done | bytes 2621456 | tf_op jit(solution)/shard_map/psum | solution.py:12
  427.7 26.0 %convolution_bitcast_fusion.1 = f32[1280,256]{0,1:T(8,128)} fusion(f32[2560,256]{1,0:T(8,128)S(1)} %bitcast.200, f32[1280,2560]{1,0:T(8,128)} %bitcast.192), kind=kOutput, calls=%fused_computation.30 | convolution fusion | flops 10066329600 | bytes 17039360 | tf_op jit(solution)/shard_map/dot_general | solution.py:16
  454.4 4.2 while.9
  459.3 20.5 %custom-call.24 = f32[2,128,128]{1,2,0:T(8,128)S(1)} custom-call(f32[2,128,128]{2,1,0:T(8,128)} %copy-done.16), custom_call_target="InvertDiagBlocksLowerTriangular" | custom-call | tf_op jit(solution)/shard_map/triangular_solve/custom-call.0 | solution.py:47
  479.8 4.4 add.167
  488.6 21.7 %all-reduce.18.cloned.1.call-done = f32[1280,256]{0,1:T(8,128)} async-done(((f32[1280,256]{0,1:T(8,128)}), f32[1280,256]{0,1:T(8,128)}) %all-reduce.18.cloned.1.call-update) | async-done | bytes 1310736 | tf_op jit(solution)/shard_map/psum | solution.py:115
  514.2 3.0 fusion.106
  520.4 114.7 %all-reduce.20.cloned.1.call-done = f32[256,256]{1,0:T(8,128)} async-done(((f32[256,256]{1,0:T(8,128)}), f32[256,256]{1,0:T(8,128)}) %all-reduce.20.cloned.1.call-update) | async-done | bytes 262160 | tf_op jit(solution)/shard_map/psum | solution.py:117
  641.9 6.9 convolution_subtract_fusion.3
  648.8 24.9 %convolution_subtract_fusion.1 = f32[1280,2560]{1,0:T(8,128)S(1)} fusion(f32[1280,2560]{1,0:T(8,128)} %bitcast.193, f32[2560,256]{1,0:T(8,128)S(1)} %bitcast.202, f32[2560,256]{1,0:T(8,128)S(1)} %convolution_subtract_fusion.3, f32[1280,256]{1,0:T(8,128)S(1)} %fusion.7, f32[1280,256]{1,0:T(8,128)S(1)} %copy-done.3), kind=kOutput, calls=%fused_computation.11 | convolution fusion | flops 20137902080 | bytes 34078720 | tf_op jit(solution)/shard_map/dot_general | solution.py:35
  673.7 4.9 copy-done
  679.8 55.5 %all-reduce.34.cloned.1.call-done = (f32[1280,128]{1,0:T(8,128)}, f32[1280,128]{1,0:T(8,128)}) async-done(((f32[1280,128]{1,0:T(8,128)}, f32[1280,128]{1,0:T(8,128)}), (f32[1280,128]{1,0:T(8,128)}, f32[1280,128]{1,0:T(8,128)})) %all-reduce.34.cloned.1.call-update) | async-done | bytes 1310736 | tf_op jit(solution)/shard_map/psum | solution.py:12
  740.9 56.6 %all-reduce.28.cloned.1.call-done = (f32[128,256]{1,0:T(8,128)}, f32[128,256]{1,0:T(8,128)}, f32[256,256]{0,1:T(8,128)}) async-done(((f32[128,256]{1,0:T(8,128)}, f32[128,256]{1,0:T(8,128)}, f32[256,256]{0,1:T(8,128)}), (f32[128,256]{1,0:T(8,128)}, f32[128,256]{1,0:T(8,128)}, f32[256,256]{0,1:T(8,128)})) %all-reduce.28.cloned.1.call-update) | async-done | bytes 524304 | tf_op jit(solution)/shard_map/psum | solution.py:12
  799.6 11.7 cholesky.282
  811.4 9.8 custom-call.25
  821.7 11.7 cholesky.299
  836.1 3.9 while.10
  840.0 19.7 %custom-call.26 = f32[2,128,128]{1,2,0:T(8,128)S(1)} custom-call(f32[2,128,128]{2,1,0:T(8,128)S(1)} %get-tuple-element.35), custom_call_target="InvertDiagBlocksLowerTriangular" | custom-call | tf_op jit(solution)/shard_map/triangular_solve/custom-call.0 | solution.py:47
  866.2 24.4 %fusion.113 = f32[2560,256]{1,0:T(8,128)S(1)} fusion(f32[1280,2560]{1,0:T(8,128)} %copy-done, f32[1280,256]{1,0:T(8,128)S(1)} %get-tuple-element.130), kind=kOutput, calls=%fused_computation.228 | convolution fusion | flops 10066329600 | bytes 17039360 | tf_op jit(solution)/shard_map/dot_general | solution.py:25
  894.2 11.7 cholesky.316
  905.9 9.8 custom-call.27
  915.8 3.8 add.169
  920.7 11.7 cholesky.333
  935.9 51.2 %all-reduce.26.cloned.1.call-done = (f32[1,10,128,256]{3,2,0,1:T(8,128)}, f32[1,10,128,256]{3,2,0,1:T(8,128)}) async-done(((f32[1,10,128,256]{3,2,0,1:T(8,128)}, f32[1,10,128,256]{3,2,0,1:T(8,128)}), (f32[1,10,128,256]{3,2,0,1:T(8,128)}, f32[1,10,128,256]{3,2,0,1:T(8,128)})) %all-reduce.26.cloned.1.call-update) | async-done | bytes 2621456 | tf_op jit(solution)/shard_map/psum | solution.py:12
  989.1 14.5 %fusion.109 = f32[1280,256]{1,0:T(8,128)} fusion(f32[1280,2560]{1,0:T(8,128)} %copy-done, f32[2560,256]{1,0:T(8,128)S(1)} %bitcast.197), kind=kOutput, calls=%fused_computation.224 | convolution fusion | flops 10066329600 | bytes 17039360 | tf_op jit(solution)/shard_map/dot_general | solution.py:16
  1003.7 4.0 while.11
  1008.4 20.9 %custom-call.28 = f32[2,128,128]{1,2,0:T(8,128)S(1)} custom-call(f32[2,128,128]{2,1,0:T(8,128)} %copy-done.15), custom_call_target="InvertDiagBlocksLowerTriangular" | custom-call | tf_op jit(solution)/shard_map/triangular_solve/custom-call.0 | solution.py:47
  1029.4 4.4 add.170
  1038.0 22.3 %all-reduce.22.cloned.1.call-done = f32[1280,256]{1,0:T(8,128)} async-done(((f32[1280,256]{1,0:T(8,128)}), f32[1280,256]{1,0:T(8,128)}) %all-reduce.22.cloned.1.call-update) | async-done | bytes 1310736 | tf_op jit(solution)/shard_map/psum | solution.py:115
  1064.2 3.0 fusion.111
  1070.1 114.5 %all-reduce.24.cloned.1.call-done = f32[256,256]{1,0:T(8,128)} async-done(((f32[256,256]{1,0:T(8,128)}), f32[256,256]{1,0:T(8,128)}) %all-reduce.24.cloned.1.call-update) | async-done | bytes 262160 | tf_op jit(solution)/shard_map/psum | solution.py:117
  1191.4 5.2 convolution_subtract_fusion.2
  1196.6 25.6 %convolution_subtract_fusion = f32[1280,2560]{1,0:T(8,128)} fusion(f32[1280,2560]{1,0:T(8,128)} %copy-done, f32[2560,256]{1,0:T(8,128)S(1)} %bitcast.199, f32[2560,256]{1,0:T(8,128)S(1)} %convolution_subtract_fusion.2, f32[1280,256]{1,0:T(8,128)S(1)} %fusion.6, f32[1280,256]{1,0:T(8,128)S(1)} %copy-done.6), kind=kOutput, calls=%fused_computation.10 | convolution fusion | flops 20137902080 | bytes 34078720 | tf_op jit(solution)/shard_map/dot_general | solution.py:35
  1222.2 19.9 %reshape.157 = f32[10,1,128,20,1,128]{5,4,3,2,1,0:T(1,128)} reshape(f32[1280,2560]{1,0:T(8,128)} %convolution_subtract_fusion) | data formatting | bytes 26214400 | tf_op jit(solution)/shard_map/reshape | solution.py:131
  (202 shorter events, 106.5 us)
Async XLA Ops:
  6.5 177.4 %all-reduce.36.cloned.1.call-start = ((), (), s32[]{:S(2)}) async-start(), calls=%async_computation.9 | async-start | bytes 2621440 | tf_op jit(solution)/shard_map/psum | solution.py:12
  124.6 121.4 %all-reduce.32.cloned.1.call-start = ((), (), s32[]{:S(2)}) async-start(), calls=%async_computation.7 | async-start | bytes 1048576 | tf_op jit(solution)/shard_map/psum | solution.py:12
  189.2 236.6 %all-reduce.30.cloned.1.call-start = ((), (), s32[]{:S(2)}) async-start(), calls=%async_computation.6 | async-start | bytes 5242880 | tf_op jit(solution)/shard_map/psum | solution.py:12
  281.9 26.8 %copy-start.17 = (f32[128,256]{1,0:T(8,128)S(1)}, f32[128,256]{1,0:T(8,128)}, u32[]{:S(2)}) copy-start(f32[128,256]{1,0:T(8,128)} %get-tuple-element.76) | copy-start | bytes 393220
  282.0 26.8 %copy-start.18 = (f32[128,256]{1,0:T(8,128)S(1)}, f32[128,256]{1,0:T(8,128)}, u32[]{:S(2)}) copy-start(f32[128,256]{1,0:T(8,128)} %get-tuple-element.77) | copy-start | bytes 393220
  288.2 19.7 %copy-start.21 = (s32[2,2]{1,0:T(2,128)}, s32[2,2]{1,0:T(2,128)S(1)}, u32[]{:S(2)}) copy-start(s32[2,2]{1,0:T(2,128)S(1)} %get-tuple-element.401) | copy-start | bytes 52
  314.4 15.1 %copy-start.1 = (f32[1280,256]{1,0:T(8,128)}, f32[1280,256]{1,0:T(8,128)S(1)}, u32[]{:S(2)}) copy-start(f32[1280,256]{1,0:T(8,128)S(1)} %get-tuple-element.125) | copy-start | bytes 3932164
  329.6 25.4 %collective-permute-start = (f32[2560,256]{0,1:T(8,128)S(1)}, f32[2560,256]{0,1:T(8,128)}, u32[]{:S(2)}, u32[]{:S(2)}) collective-permute-start(f32[2560,256]{0,1:T(8,128)S(1)} %convolution_bitcast_fusion), channel_id=1, source_target_pairs={{0,4},{4,0},{8,12},{12,8},{16,20},{20,16},{24,28},{28,24},{1,5},{5... | collective-permute-start | bytes 7864328 | tf_op jit(solution)/shard_map/ppermute | solution.py:123
  331.2 179.2 %all-reduce.18.cloned.1.call-start = ((), (), s32[]{:S(2)}) async-start(), calls=%async_computation | async-start | bytes 2621440 | tf_op jit(solution)/shard_map/psum | solution.py:115
  332.6 0.7 copy-start.11
  354.9 4.4 copy-start.12
  358.8 121.0 %collective-permute-start.1 = (f32[2560,256]{0,1:T(8,128)}, f32[2560,256]{0,1:T(8,128)}, u32[]{:S(2)}, u32[]{:S(2)}) collective-permute-start(f32[2560,256]{0,1:T(8,128)} %add.166), channel_id=1, source_target_pairs={{0,8},{4,12},{8,0},{12,4},{16,24},{20,28},{24,16},{28,20},{1,9},{5... | collective-permute-start | bytes 7864328 | tf_op jit(solution)/shard_map/ppermute | solution.py:123
  371.6 2.5 copy-start.9
  453.8 0.7 copy-start.22
  453.8 181.3 %all-reduce.20.cloned.1.call-start = ((), (), s32[]{:S(2)}) async-start(), calls=%async_computation.1 | async-start | bytes 524288 | tf_op jit(solution)/shard_map/psum | solution.py:117
  458.6 0.7 copy-start.16
  484.2 157.6 %collective-permute-start.2 = (f32[2560,256]{0,1:T(8,128)}, f32[2560,256]{0,1:T(8,128)}, u32[]{:S(2)}, u32[]{:S(2)}) collective-permute-start(f32[2560,256]{0,1:T(8,128)} %add.167), channel_id=1, source_target_pairs={{0,16},{4,20},{8,24},{12,28},{16,0},{20,4},{24,8},{28,12},{1,17},{... | collective-permute-start | bytes 7864328 | tf_op jit(solution)/shard_map/ppermute | solution.py:123
  510.4 3.9 copy-start.2
  513.1 1.1 copy-start.7
  517.3 218.1 %all-reduce.34.cloned.1.call-start = ((), (), s32[]{:S(2)}) async-start(), calls=%async_computation.8 | async-start | bytes 2621440 | tf_op jit(solution)/shard_map/psum | solution.py:12
  641.8 6.9 copy-start.3
  673.6 5.0 copy-start
  679.8 117.7 %all-reduce.28.cloned.1.call-start = ((), (), s32[]{:S(2)}) async-start(), calls=%async_computation.5 | async-start | bytes 1048576 | tf_op jit(solution)/shard_map/psum | solution.py:12
  740.6 246.5 %all-reduce.26.cloned.1.call-start = ((), (), s32[]{:S(2)}) async-start(), calls=%async_computation.4 | async-start | bytes 5242880 | tf_op jit(solution)/shard_map/psum | solution.py:12
  833.4 27.1 %copy-start.19 = (f32[128,256]{1,0:T(8,128)S(1)}, f32[128,256]{1,0:T(8,128)}, u32[]{:S(2)}) copy-start(f32[128,256]{1,0:T(8,128)} %get-tuple-element.71) | copy-start | bytes 393220
  833.4 27.1 %copy-start.20 = (f32[128,256]{1,0:T(8,128)S(1)}, f32[128,256]{1,0:T(8,128)}, u32[]{:S(2)}) copy-start(f32[128,256]{1,0:T(8,128)} %get-tuple-element.72) | copy-start | bytes 393220
  866.2 24.4 %copy-start.4 = (f32[1280,256]{1,0:T(8,128)}, f32[1280,256]{1,0:T(8,128)S(1)}, u32[]{:S(2)}) copy-start(f32[1280,256]{1,0:T(8,128)S(1)} %get-tuple-element.130) | copy-start | bytes 3932164
  890.6 25.2 %collective-permute-start.3 = (f32[2560,256]{1,0:T(8,128)S(1)}, f32[2560,256]{1,0:T(8,128)}, u32[]{:S(2)}, u32[]{:S(2)}) collective-permute-start(f32[2560,256]{1,0:T(8,128)S(1)} %fusion.113), channel_id=1, source_target_pairs={{0,4},{4,0},{8,12},{12,8},{16,20},{20,16},{24,28},{28,24},{1,5},{5... | collective-permute-start | bytes 7864328 | tf_op jit(solution)/shard_map/ppermute | solution.py:123
  892.2 168.1 %all-reduce.22.cloned.1.call-start = ((), (), s32[]{:S(2)}) async-start(), calls=%async_computation.2 | async-start | bytes 2621440 | tf_op jit(solution)/shard_map/psum | solution.py:115
  893.4 0.7 copy-start.13
  915.7 4.4 copy-start.14
  919.5 109.8 %collective-permute-start.4 = (f32[2560,256]{1,0:T(8,128)}, f32[2560,256]{1,0:T(8,128)}, u32[]{:S(2)}, u32[]{:S(2)}) collective-permute-start(f32[2560,256]{1,0:T(8,128)} %add.169), channel_id=1, source_target_pairs={{0,8},{4,12},{8,0},{12,4},{16,24},{20,28},{24,16},{28,20},{1,9},{5... | collective-permute-start | bytes 7864328 | tf_op jit(solution)/shard_map/ppermute | solution.py:123
  932.4 2.5 copy-start.10
  1003.7 180.9 %all-reduce.24.cloned.1.call-start = ((), (), s32[]{:S(2)}) async-start(), calls=%async_computation.3 | async-start | bytes 524288 | tf_op jit(solution)/shard_map/psum | solution.py:117
  1007.8 0.7 copy-start.15
  1033.8 157.6 %collective-permute-start.5 = (f32[2560,256]{1,0:T(8,128)}, f32[2560,256]{1,0:T(8,128)}, u32[]{:S(2)}, u32[]{:S(2)}) collective-permute-start(f32[2560,256]{1,0:T(8,128)} %add.170), channel_id=1, source_target_pairs={{0,16},{4,20},{8,24},{12,28},{16,0},{20,4},{24,8},{28,12},{1,17},{... | collective-permute-start | bytes 7864328 | tf_op jit(solution)/shard_map/ppermute | solution.py:123
  1060.4 3.9 copy-start.5
  1063.1 1.1 copy-start.8
  1191.4 5.2 copy-start.6
Sparse Core Ops, SparseCore 0:
  124.8 59.0 all-reduce.35
  189.3 56.7 all-reduce.31
  331.3 94.4 all-reduce.29
  453.9 56.3 all-reduce.17
  517.4 117.7 all-reduce.19
  679.9 55.4 all-reduce.33
  740.8 56.7 all-reduce.27
  892.3 94.7 all-reduce.25
  1003.8 56.5 all-reduce.21
  1067.4 117.1 all-reduce.23
